TPU v7x, 32 devices: a whole 2x2x4 slice. The times are simulated.
32 devices in a mesh: rep: 4 (over y, core), shard: 4 (over z), ctx: 2 (over x).
Axes of the slice: x: 2, y: 2, z: 4, core: 2. Of those that a mesh axis runs over, the one named last changes fastest.
Arguments:
- tokens: bfloat16 [2, 4, 512, 2048], P(None, 'rep', ('shard', 'ctx')), may hold values from -6 to 6
- span_starts: int32 [2, 4], P(None, 'rep'), may hold values from 0 to 256
- cotangent: bfloat16 [2, 4, 512, 2048], P(None, 'rep', ('shard', 'ctx')), may hold values from -6 to 6
- w_query: bfloat16 [2048, 2048], P('shard'), may hold values from -0.125 to 0.125
- key_weight: bfloat16 [2048, 1024], P('shard'), may hold values from -0.125 to 0.125
- value_weight: bfloat16 [2048, 1024], P('shard'), may hold values from -0.125 to 0.125
- w_out: bfloat16 [2048, 2048], P('shard'), may hold values from -0.75 to 0.75
- attn_gain: bfloat16 [2048], P('shard'), may hold values from 0.099609375 to 1.8984375
- query_gain: bfloat16 [128], P('shard'), may hold values from 0.099609375 to 1.8984375
- key_gain: bfloat16 [128], P('shard'), may hold values from 0.099609375 to 1.8984375
- w_gate: bfloat16 [2048, 6144], P('shard'), may hold values from -0.125 to 0.125
- w_up: bfloat16 [2048, 6144], P('shard'), may hold values from -0.125 to 0.125
- w_down: bfloat16 [6144, 2048], P('shard'), may hold values from -0.078125 to 0.078125
- ffn_gain: bfloat16 [2048], P('shard'), may hold values from 0.099609375 to 1.8984375
Outputs:
- output: bfloat16 [2, 4, 512, 2048], P(None, 'rep', ('shard', 'ctx'))
- input_grad: float32 [2, 4, 512, 2048], P(None, 'rep', ('shard', 'ctx'))
- grad_query: float32 [2048, 2048], P('shard')
- grad_key: float32 [2048, 1024], P('shard')
- grad_value: float32 [2048, 1024], P('shard')
- grad_out: float32 [2048, 2048], P('shard')
- grad_attn_gain: float32 [2048], P('shard')
- grad_query_gain: float32 [128], P('shard')
- grad_key_gain: float32 [128], P('shard')
- grad_gate: float32 [2048, 6144], P('shard')
- grad_up: float32 [2048, 6144], P('shard')
- grad_down: float32 [6144, 2048], P('shard')
- grad_ffn_gain: float32 [2048], P('shard')
Inputs may be any that keep to these rules, and one draw needn't show every extreme that they name: `span_starts`: each sequence's picture span covers positions start to start + 255 of that sequence.
All inputs are finite; a program needn't handle non-finite values.
Results may differ from a plain program's by a relative error of at most 0.023.
Values may be sent and summed in bfloat16 or wider, within the bound.
No kernel may reach another device: no remote copies, remote signals or barrier semaphores. Data moves between devices by JAX's collectives and lax.ppermute only.
A program may use at most 448 MiB of HBM per device.

v0:
```python
from functools import partial
import jax
import jax.numpy as jnp
from jax import lax
from jax.sharding import PartitionSpec as P

QUERY_HEADS = 16
KEY_VALUE_HEADS = 8
HEAD_SIZE = 128
PIC = 256
EPSILON = 1e-06
THETA = 1000000.0


def apply_rotation(values):
    half_width = values.shape[-1] // 2
    return jnp.concatenate([-values[..., half_width:], values[..., :half_width]], axis=-1)


def rotate_back(values):
    half_width = values.shape[-1] // 2
    return jnp.concatenate([values[..., half_width:], -values[..., :half_width]], axis=-1)


def spin_tables(positions):
    inverse = THETA ** (-jnp.arange(HEAD_SIZE // 2, dtype=jnp.float32) * 2.0 / HEAD_SIZE)
    angles = positions.astype(jnp.float32)[:, None] * inverse[None, :]
    cosine_table = jnp.concatenate([jnp.cos(angles), jnp.cos(angles)], axis=-1)[:, None, :]
    sine_values = jnp.concatenate([jnp.sin(angles), jnp.sin(angles)], axis=-1)[:, None, :]
    return (cosine_table, sine_values)


def recip_rms(values):
    return lax.rsqrt(jnp.mean(values * values, axis=-1, keepdims=True) + EPSILON)


def norm_back(unit, recip, gain, d_normed):
    d_unit = d_normed * gain
    return recip * (d_unit - unit * jnp.mean(d_unit * unit, axis=-1, keepdims=True))


def over_rows(left, right):
    return lax.dot_general(
        left, right, (((0,), (0,)), ((), ())), preferred_element_type=jnp.float32
    )


def compared_to(left, right):
    return lax.dot_general(
        left, right, (((1,), (1,)), ((), ())), preferred_element_type=jnp.float32
    )


def attention_set(w_query, key_weight, value_weight, w_out, attn_gain, query_gain, key_gain):
    return (
        lax.all_gather(w_query, "shard", axis=0, tiled=True),
        lax.all_gather(key_weight, "shard", axis=0, tiled=True),
        lax.all_gather(value_weight, "shard", axis=0, tiled=True),
        lax.all_gather(w_out, "shard", axis=0, tiled=True),
        lax.all_gather(attn_gain, "shard", axis=0, tiled=True),
        lax.all_gather(query_gain, "shard", axis=0, tiled=True),
        lax.all_gather(key_gain, "shard", axis=0, tiled=True),
    )


def feedforward_set(w_gate, w_up, w_down, ffn_gain):
    return (
        lax.all_gather(w_gate, "shard", axis=0, tiled=True),
        lax.all_gather(w_up, "shard", axis=0, tiled=True),
        lax.all_gather(w_down, "shard", axis=0, tiled=True),
        lax.all_gather(ffn_gain, "shard", axis=0, tiled=True),
    )


def masked_scores(allowed, q_head, k_head):
    scores = jnp.einsum(
        "tgd,sd->gts", q_head, k_head, preferred_element_type=jnp.float32
    ) * HEAD_SIZE ** (-0.5)
    return jnp.where(allowed, scores, -1e30)


def head_forward(allowed, pieces):
    q_head, k_head, v_head = pieces
    scores = masked_scores(allowed, q_head, k_head)
    highest = jnp.max(scores, axis=-1, keepdims=True)
    log_total = highest + jnp.log(jnp.sum(jnp.exp(scores - highest), axis=-1, keepdims=True))
    probs_low = jnp.exp(scores - log_total).astype(jnp.bfloat16)
    mixed = jnp.einsum("gts,sd->tgd", probs_low, v_head, preferred_element_type=jnp.float32)
    return (mixed, log_total)


def head_backward(allowed, pieces):
    q_head, k_head, v_head, d_mix_head, log_total = pieces
    probs = jnp.exp(masked_scores(allowed, q_head, k_head) - log_total)
    probs_low = probs.astype(jnp.bfloat16)
    d_probs = jnp.einsum("tgd,sd->gts", d_mix_head, v_head, preferred_element_type=jnp.float32)
    d_values = jnp.einsum("gts,tgd->sd", probs_low, d_mix_head, preferred_element_type=jnp.float32)
    row_dot = jnp.sum(probs * d_probs, axis=-1, keepdims=True)
    d_scores = (probs * (d_probs - row_dot)).astype(jnp.bfloat16)
    d_queries = jnp.einsum(
        "gts,sd->tgd", d_scores, k_head, preferred_element_type=jnp.float32
    ) * HEAD_SIZE ** (-0.5)
    d_keys = jnp.einsum(
        "gts,tgd->sd", d_scores, q_head, preferred_element_type=jnp.float32
    ) * HEAD_SIZE ** (-0.5)
    return (d_queries, d_keys, d_values)


def shards(
    tokens,
    span_starts,
    cotangent,
    w_query,
    key_weight,
    value_weight,
    w_out,
    attn_gain,
    query_gain,
    key_gain,
    w_gate,
    w_up,
    w_down,
    ffn_gain,
):
    seq_count = lax.axis_size(("shard", "ctx"))
    seq_rank = lax.axis_index(("shard", "ctx"))
    token_rows = tokens.shape[2]
    token_length = token_rows * seq_count
    group_width = QUERY_HEADS // KEY_VALUE_HEADS
    local_pos = seq_rank * token_rows + jnp.arange(token_rows, dtype=jnp.int32)
    key_pos = jnp.arange(token_length, dtype=jnp.int32)
    cosine_table, sine_values = spin_tables(local_pos)
    cos_keys = cosine_table[:, 0, :][None]
    sin_keys = sine_values[:, 0, :][None]
    out_list = []
    grad_list = []
    stored = []
    totals = None
    for micro_index in range(tokens.shape[0]):
        span_start = span_starts[micro_index, 0]
        inside_q = (local_pos >= span_start) & (local_pos < span_start + PIC)
        inside_k = (key_pos >= span_start) & (key_pos < span_start + PIC)
        allowed = (key_pos[None, :] <= local_pos[:, None]) | inside_q[:, None] & inside_k[None, :]
        hidden_in = tokens[micro_index, 0].astype(jnp.float32)
        full_query, full_key, full_value, complete_output, gain_attn, gain_query, gain_key = (
            attention_set(w_query, key_weight, value_weight, w_out, attn_gain, query_gain, key_gain)
        )
        gain_attn = gain_attn.astype(jnp.float32)
        gain_query = gain_query.astype(jnp.float32)
        gain_key = gain_key.astype(jnp.float32)
        recip_h = recip_rms(hidden_in)
        unit_h = hidden_in * recip_h
        normalized_rows = (unit_h * gain_attn).astype(jnp.bfloat16)
        q_pre = jnp.dot(normalized_rows, full_query, preferred_element_type=jnp.float32).reshape(
            token_rows, QUERY_HEADS, HEAD_SIZE
        )
        key_before_rotation = jnp.transpose(
            jnp.dot(normalized_rows, full_key, preferred_element_type=jnp.float32).reshape(
                token_rows, KEY_VALUE_HEADS, HEAD_SIZE
            ),
            (1, 0, 2),
        )
        value_local = jnp.transpose(
            jnp.dot(normalized_rows, full_value, preferred_element_type=jnp.float32)
            .astype(jnp.bfloat16)
            .reshape(token_rows, KEY_VALUE_HEADS, HEAD_SIZE),
            (1, 0, 2),
        )
        recip_q = recip_rms(q_pre)
        unit_query = q_pre * recip_q
        recip_k = recip_rms(key_before_rotation)
        unit_k = key_before_rotation * recip_k
        scaled_q = unit_query * gain_query
        scaled_k = unit_k * gain_key
        query_rows = jnp.transpose(
            (scaled_q * cosine_table + apply_rotation(scaled_q) * sine_values)
            .astype(jnp.bfloat16)
            .reshape(token_rows, KEY_VALUE_HEADS, group_width, HEAD_SIZE),
            (1, 0, 2, 3),
        )
        key_local = (scaled_k * cos_keys + apply_rotation(scaled_k) * sin_keys).astype(jnp.bfloat16)
        key_rows, value_matrix = (
            lax.all_gather(key_local, ("shard", "ctx"), axis=1, tiled=True),
            lax.all_gather(value_local, ("shard", "ctx"), axis=1, tiled=True),
        )
        mixed_split, log_total = lax.map(
            partial(head_forward, allowed), (query_rows, key_rows, value_matrix)
        )
        mixed_heads = (
            jnp.transpose(mixed_split, (1, 0, 2, 3))
            .reshape(token_rows, QUERY_HEADS * HEAD_SIZE)
            .astype(jnp.bfloat16)
        )
        middle = hidden_in + jnp.dot(
            mixed_heads, complete_output, preferred_element_type=jnp.float32
        )
        full_gate, full_up, full_down, gain_ffn = feedforward_set(w_gate, w_up, w_down, ffn_gain)
        gain_ffn = gain_ffn.astype(jnp.float32)
        recip_m = recip_rms(middle)
        unit_m = middle * recip_m
        ffn_in = (unit_m * gain_ffn).astype(jnp.bfloat16)
        gate_pre = jnp.dot(ffn_in, full_gate, preferred_element_type=jnp.float32)
        up_pre = jnp.dot(ffn_in, full_up, preferred_element_type=jnp.float32)
        sigma = jax.nn.sigmoid(gate_pre)
        act_gate = gate_pre * sigma
        inner_act = (act_gate * up_pre).astype(jnp.bfloat16)
        result = middle + jnp.dot(inner_act, full_down, preferred_element_type=jnp.float32)
        out_list.append(result.astype(jnp.bfloat16))
        cot_rows = cotangent[micro_index, 0]
        cot_float = cot_rows.astype(jnp.float32)
        d_inner = compared_to(cot_rows, full_down)
        d_gate = (d_inner * up_pre * sigma * (1.0 + gate_pre * (1.0 - sigma))).astype(jnp.bfloat16)
        d_up = (d_inner * act_gate).astype(jnp.bfloat16)
        d_ffn_in = compared_to(d_gate, full_gate) + compared_to(d_up, full_up)
        ffn_gain_part = jnp.sum(d_ffn_in * unit_m, axis=0)
        d_middle = cot_float + norm_back(unit_m, recip_m, gain_ffn, d_ffn_in)
        branch_gradient = d_middle.astype(jnp.bfloat16)
        d_mixed = jnp.transpose(
            compared_to(branch_gradient, complete_output)
            .astype(jnp.bfloat16)
            .reshape(token_rows, KEY_VALUE_HEADS, group_width, HEAD_SIZE),
            (1, 0, 2, 3),
        )
        d_split_q, d_keys, d_values = lax.map(
            partial(head_backward, allowed),
            (query_rows, key_rows, value_matrix, d_mixed, log_total),
        )
        d_queries = jnp.transpose(d_split_q, (1, 0, 2, 3)).reshape(
            token_rows, QUERY_HEADS, HEAD_SIZE
        )
        d_key_local, d_value_local = (
            lax.psum_scatter(
                d_keys.astype(jnp.bfloat16), ("shard", "ctx"), scatter_dimension=1, tiled=True
            ).astype(jnp.float32),
            lax.psum_scatter(
                d_values.astype(jnp.bfloat16), ("shard", "ctx"), scatter_dimension=1, tiled=True
            ).astype(jnp.float32),
        )
        d_unit_q = d_queries * cosine_table + rotate_back(d_queries * sine_values)
        d_unit_k = d_key_local * cos_keys + rotate_back(d_key_local * sin_keys)
        query_gain_part = jnp.sum(d_unit_q * unit_query, axis=(0, 1))
        key_gain_part = jnp.sum(d_unit_k * unit_k, axis=(0, 1))
        d_q_pre = (
            norm_back(unit_query, recip_q, gain_query, d_unit_q)
            .astype(jnp.bfloat16)
            .reshape(token_rows, QUERY_HEADS * HEAD_SIZE)
        )
        d_k_pre = jnp.transpose(
            norm_back(unit_k, recip_k, gain_key, d_unit_k).astype(jnp.bfloat16), (1, 0, 2)
        ).reshape(token_rows, KEY_VALUE_HEADS * HEAD_SIZE)
        d_v_pre = jnp.transpose(d_value_local.astype(jnp.bfloat16), (1, 0, 2)).reshape(
            token_rows, KEY_VALUE_HEADS * HEAD_SIZE
        )
        d_normed = (
            compared_to(d_q_pre, full_query)
            + compared_to(d_k_pre, full_key)
            + compared_to(d_v_pre, full_value)
        )
        attn_gain_part = jnp.sum(d_normed * unit_h, axis=0)
        grad_list.append(d_middle + norm_back(unit_h, recip_h, gain_attn, d_normed))
        stored.append(
            (
                normalized_rows,
                d_q_pre,
                d_k_pre,
                d_v_pre,
                mixed_heads,
                branch_gradient,
                ffn_in,
                d_gate,
                d_up,
                inner_act,
                cot_rows,
            )
        )
        parts = (attn_gain_part, query_gain_part, key_gain_part, ffn_gain_part)
        if totals is None:
            totals = parts
        else:
            totals = tuple((older + newer for older, newer in zip(totals, parts)))
    joined = [
        jnp.concatenate([saved_set[member] for saved_set in stored], axis=0) for member in range(11)
    ]
    (
        normed_all,
        dq_all,
        dk_all,
        dv_all,
        mixed_all,
        branch_all,
        ffn_all,
        gate_all,
        up_all,
        inner_all,
        cot_all,
    ) = joined
    totals = (
        lax.psum_scatter(
            over_rows(normed_all, dq_all).astype(jnp.bfloat16),
            "shard",
            scatter_dimension=0,
            tiled=True,
        ).astype(jnp.float32),
        lax.psum_scatter(
            over_rows(normed_all, dk_all).astype(jnp.bfloat16),
            "shard",
            scatter_dimension=0,
            tiled=True,
        ).astype(jnp.float32),
        lax.psum_scatter(
            over_rows(normed_all, dv_all).astype(jnp.bfloat16),
            "shard",
            scatter_dimension=0,
            tiled=True,
        ).astype(jnp.float32),
        lax.psum_scatter(
            over_rows(mixed_all, branch_all).astype(jnp.bfloat16),
            "shard",
            scatter_dimension=0,
            tiled=True,
        ).astype(jnp.float32),
        lax.psum_scatter(
            totals[0].astype(jnp.bfloat16), "shard", scatter_dimension=0, tiled=True
        ).astype(jnp.float32),
        lax.psum_scatter(
            totals[1].astype(jnp.bfloat16), "shard", scatter_dimension=0, tiled=True
        ).astype(jnp.float32),
        lax.psum_scatter(
            totals[2].astype(jnp.bfloat16), "shard", scatter_dimension=0, tiled=True
        ).astype(jnp.float32),
        lax.psum_scatter(
            over_rows(ffn_all, gate_all).astype(jnp.bfloat16),
            "shard",
            scatter_dimension=0,
            tiled=True,
        ).astype(jnp.float32),
        lax.psum_scatter(
            over_rows(ffn_all, up_all).astype(jnp.bfloat16),
            "shard",
            scatter_dimension=0,
            tiled=True,
        ).astype(jnp.float32),
        lax.psum_scatter(
            over_rows(inner_all, cot_all).astype(jnp.bfloat16),
            "shard",
            scatter_dimension=0,
            tiled=True,
        ).astype(jnp.float32),
        lax.psum_scatter(
            totals[3].astype(jnp.bfloat16), "shard", scatter_dimension=0, tiled=True
        ).astype(jnp.float32),
    )
    summed = (
        lax.psum(totals[0].astype(jnp.bfloat16), ("rep", "ctx")).astype(jnp.float32),
        lax.psum(totals[1].astype(jnp.bfloat16), ("rep", "ctx")).astype(jnp.float32),
        lax.psum(totals[2].astype(jnp.bfloat16), ("rep", "ctx")).astype(jnp.float32),
        lax.psum(totals[3].astype(jnp.bfloat16), ("rep", "ctx")).astype(jnp.float32),
        lax.psum(totals[4].astype(jnp.bfloat16), ("rep", "ctx")).astype(jnp.float32),
        lax.psum(totals[5].astype(jnp.bfloat16), ("rep", "ctx")).astype(jnp.float32),
        lax.psum(totals[6].astype(jnp.bfloat16), ("rep", "ctx")).astype(jnp.float32),
        lax.psum(totals[7].astype(jnp.bfloat16), ("rep", "ctx")).astype(jnp.float32),
        lax.psum(totals[8].astype(jnp.bfloat16), ("rep", "ctx")).astype(jnp.float32),
        lax.psum(totals[9].astype(jnp.bfloat16), ("rep", "ctx")).astype(jnp.float32),
        lax.psum(totals[10].astype(jnp.bfloat16), ("rep", "ctx")).astype(jnp.float32),
    )
    output = jnp.stack(out_list)[:, None]
    input_grad = jnp.stack(grad_list)[:, None]
    return (
        output,
        input_grad,
        summed[0],
        summed[1],
        summed[2],
        summed[3],
        summed[4],
        summed[5],
        summed[6],
        summed[7],
        summed[8],
        summed[9],
        summed[10],
    )


def solution(mesh):
    in_specs = (
        P(None, "rep", ("shard", "ctx"), None),
        P(None, "rep"),
        P(None, "rep", ("shard", "ctx"), None),
        P("shard", None),
        P("shard", None),
        P("shard", None),
        P("shard", None),
        P("shard"),
        P("shard"),
        P("shard"),
        P("shard", None),
        P("shard", None),
        P("shard", None),
        P("shard"),
    )
    out_specs = (
        P(None, "rep", ("shard", "ctx"), None),
        P(None, "rep", ("shard", "ctx"), None),
        P("shard", None),
        P("shard", None),
        P("shard", None),
        P("shard", None),
        P("shard"),
        P("shard"),
        P("shard"),
        P("shard", None),
        P("shard", None),
        P("shard", None),
        P("shard"),
    )
    return jax.shard_map(shards, mesh=mesh, in_specs=in_specs, out_specs=out_specs, check_vma=False)
```

profile of v0, /device:TPU:0, one launch (start us, length us, event | category | flops | bytes accessed | tf_op | source)
XLA Modules:
  0.0 4428.3 jit_solution(448300715896860769)
XLA Ops:
  36.3 57.1 %all-gather.18.cloned.1.call-done = bf16[2048,1024]{1,0:T(8,128)(2,1)} async-done(((bf16[512,1024]{1,0:T(8,128)(2,1)}), bf16[2048,1024]{1,0:T(8,128)(2,1)}) %all-gather.18.cloned.1.call-update) | async-done | bytes 4194320 | tf_op jit(solution)/shard_map/all_gather | solution.py:57
  108.0 66.2 %all-gather.14.cloned.1.call-done = bf16[2048,1024]{1,0:T(8,128)(2,1)} async-done(((bf16[512,1024]{1,0:T(8,128)(2,1)}), bf16[2048,1024]{1,0:T(8,128)(2,1)}) %all-gather.14.cloned.1.call-update) | async-done | bytes 4194320 | tf_op jit(solution)/shard_map/all_gather | solution.py:58
  204.3 119.9 %all-gather.22.cloned.1.call-done = bf16[2048,2048]{1,0:T(8,128)(2,1)} async-done(((bf16[512,2048]{1,0:T(8,128)(2,1)}), bf16[2048,2048]{1,0:T(8,128)(2,1)}) %all-gather.22.cloned.1.call-update) | async-done | bytes 8388624 | tf_op jit(solution)/shard_map/all_gather | solution.py:56
  365.2 41.6 all-gather.16.cloned.1.call-done
  406.8 21.4 while.56
  429.4 19.0 all-gather.34.cloned.1.call-done
  448.4 41.7 all-gather.32.cloned.1.call-done
  490.2 21.6 while.57
  512.4 127.8 %all-gather.24.cloned.1.call-done = bf16[2048,2048]{1,0:T(8,128)(2,1)} async-done(((bf16[512,2048]{1,0:T(8,128)(2,1)}), bf16[2048,2048]{1,0:T(8,128)(2,1)}) %all-gather.24.cloned.1.call-update) | async-done | bytes 8388624 | tf_op jit(solution)/shard_map/all_gather | solution.py:59
  647.8 417.4 %all-gather.26.cloned.1.call-done = bf16[2048,6144]{1,0:T(8,128)(2,1)} async-done(((bf16[512,6144]{1,0:T(8,128)(2,1)}), bf16[2048,6144]{1,0:T(8,128)(2,1)}) %all-gather.26.cloned.1.call-update) | async-done | bytes 25165840 | tf_op jit(solution)/shard_map/all_gather | solution.py:68
  1078.3 411.7 %all-gather.28.cloned.1.call-done = bf16[2048,6144]{1,0:T(8,128)(2,1)} async-done(((bf16[512,6144]{1,0:T(8,128)(2,1)}), bf16[2048,6144]{1,0:T(8,128)(2,1)}) %all-gather.28.cloned.1.call-update) | async-done | bytes 25165840 | tf_op jit(solution)/shard_map/all_gather | solution.py:69
  1503.4 411.6 %all-gather.30.cloned.1.call-done = bf16[6144,2048]{1,0:T(8,128)(2,1)} async-done(((bf16[1536,2048]{1,0:T(8,128)(2,1)}), bf16[6144,2048]{1,0:T(8,128)(2,1)}) %all-gather.30.cloned.1.call-update) | async-done | bytes 25165840 | tf_op jit(solution)/shard_map/all_gather | solution.py:70
  2033.3 55.3 %while.59 = (s32[]{:T(128)}, f32[8,64,2,128]{3,1,2,0:T(8,128)S(1)}, bf16[8,512,128]{2,1,0:T(8,128)(2,1)}, bf16[8,512,128]{2,1,0:T(8,128)(2,1)}, bf16[8,512,128]{...) while((s32[]{:T(128)}, f32[8,64,2,128]{3,1,2,0:T(8,128)S(1)}, ...), condition=%wide.region_28.29_spmd.clone, body=%wide.region_26.28_spmd.clone.sunk | while | flops 84656000 | bytes 3154369 | solution.py:224
  2102.3 60.2 %while.58 = (s32[]{:T(128)}, f32[8,64,2,128]{3,1,2,0:T(8,128)}, bf16[8,512,128]{2,1,0:T(8,128)(2,1)}, bf16[8,512,128]{2,1,0:T(8,128)(2,1)}, bf16[8,512,128]{2,1,...) while((s32[]{:T(128)}, f32[8,64,2,128]{3,1,2,0:T(8,128)}, ...), condition=%wide.region_19.20_spmd.clone, body=%wide.region_17.19_spmd.clone.sunk | while | flops 84656000 | bytes 3154369 | solution.py:224
  2165.4 63.3 %reduce-scatter.14.cloned.1.call-done = bf16[8,64,128]{2,1,0:T(8,128)(2,1)} async-done(((bf16[8,512,128]{2,1,0:T(8,128)(2,1)}), bf16[8,64,128]{2,1,0:T(8,128)(2,1)}) %reduce-scatter.14.cloned.1.call-update) | async-done | bytes 131088 | tf_op jit(solution)/shard_map/reduce_scatter | solution.py:235
  2234.1 61.2 %reduce-scatter.16.cloned.1.call-done = bf16[8,64,128]{2,1,0:T(8,128)(2,1)} async-done(((bf16[8,512,128]{2,1,0:T(8,128)(2,1)}), bf16[8,64,128]{2,1,0:T(8,128)(2,1)}) %reduce-scatter.16.cloned.1.call-update) | async-done | bytes 131088 | tf_op jit(solution)/shard_map/reduce_scatter | solution.py:232
  2295.3 67.1 %reduce-scatter.12.cloned.1.call-done = bf16[8,64,128]{2,1,0:T(8,128)(2,1)} async-done(((bf16[8,512,128]{2,1,0:T(8,128)(2,1)}), bf16[8,64,128]{2,1,0:T(8,128)(2,1)}) %reduce-scatter.12.cloned.1.call-update) | async-done | bytes 131088 | tf_op jit(solution)/shard_map/reduce_scatter | solution.py:232
  2440.9 80.1 %reduce-scatter.22.cloned.1.call-done = bf16[512,1024]{1,0:T(8,128)(2,1)} async-done(((bf16[2048,1024]{1,0:T(8,128)(2,1)}), bf16[512,1024]{1,0:T(8,128)(2,1)}) %reduce-scatter.22.cloned.1.call-update) | async-done | bytes 1048592 | tf_op jit(solution)/shard_map/reduce_scatter | solution.py:304
  2521.0 147.8 %reduce-scatter.26.cloned.1.call-done = bf16[512,2048]{1,0:T(8,128)(2,1)} async-done(((bf16[2048,2048]{1,0:T(8,128)(2,1)}), bf16[512,2048]{1,0:T(8,128)(2,1)}) %reduce-scatter.26.cloned.1.call-update) | async-done | bytes 2097168 | tf_op jit(solution)/shard_map/reduce_scatter | solution.py:316
  2668.8 148.2 %reduce-scatter.20.cloned.1.call-done = bf16[512,2048]{1,0:T(8,128)(2,1)} async-done(((bf16[2048,2048]{1,0:T(8,128)(2,1)}), bf16[512,2048]{1,0:T(8,128)(2,1)}) %reduce-scatter.20.cloned.1.call-update) | async-done | bytes 2097168 | tf_op jit(solution)/shard_map/reduce_scatter | solution.py:298
  2816.9 417.4 %reduce-scatter.30.cloned.1.call-done = bf16[512,6144]{1,0:T(8,128)(2,1)} async-done(((bf16[2048,6144]{1,0:T(8,128)(2,1)}), bf16[512,6144]{1,0:T(8,128)(2,1)}) %reduce-scatter.30.cloned.1.call-update) | async-done | bytes 6291472 | tf_op jit(solution)/shard_map/reduce_scatter | solution.py:337
  3234.3 418.7 %reduce-scatter.28.cloned.1.call-done = bf16[512,6144]{1,0:T(8,128)(2,1)} async-done(((bf16[2048,6144]{1,0:T(8,128)(2,1)}), bf16[512,6144]{1,0:T(8,128)(2,1)}) %reduce-scatter.28.cloned.1.call-update) | async-done | bytes 6291472 | tf_op jit(solution)/shard_map/reduce_scatter | solution.py:331
  3653.0 418.6 %reduce-scatter.32.cloned.1.call-done = bf16[1536,2048]{1,0:T(8,128)(2,1)} async-done(((bf16[6144,2048]{1,0:T(8,128)(2,1)}), bf16[1536,2048]{1,0:T(8,128)(2,1)}) %reduce-scatter.32.cloned.1.call-update) | async-done | bytes 6291472 | tf_op jit(solution)/shard_map/reduce_scatter | solution.py:343
  4143.1 248.2 %all-reduce.12.cloned.1.call-done = (bf16[512,2048]{1,0:T(8,128)(2,1)}, bf16[512,1024]{1,0:T(8,128)(2,1)}, bf16[512,1024]{1,0:T(8,128)(2,1)}, bf16[512,2048]{1,0...) async-done(((bf16[512,2048]{1,0:T(8,128)(2,1)}, bf16[512,1024]{1,0:T(8,128)(2,1)}, bf16[512,1024]{1,0:T(8,128)(2,1)}, ...) | async-done | bytes 25165840 | tf_op jit(solution)/shard_map/psum | solution.py:354
  (625 shorter events, 623.5 us)
Async XLA Ops:
  7.2 86.1 %all-gather.18.cloned.1.call-start = ((), (), s32[]{:S(2)}) async-start(), calls=%async_computation.13 | async-start | bytes 5242880 | tf_op jit(solution)/shard_map/all_gather | solution.py:57
  8.0 166.3 %all-gather.14.cloned.1.call-start = ((), (), s32[]{:S(2)}) async-start(), calls=%async_computation.11 | async-start | bytes 5242880 | tf_op jit(solution)/shard_map/all_gather | solution.py:58
  8.7 315.4 %all-gather.22.cloned.1.call-start = ((), (), s32[]{:S(2)}) async-start(), calls=%async_computation.15 | async-start | bytes 10485760 | tf_op jit(solution)/shard_map/all_gather | solution.py:56
  9.5 355.8 %all-gather.20.cloned.1.call-start = ((), (), s32[]{:S(2)}) async-start(), calls=%async_computation.14 | async-start | bytes 1179648 | tf_op jit(solution)/shard_map/all_gather | solution.py:183
  36.0 2327.7 %copy-start.56 = (f32[64,128]{1,0:T(8,128)}, f32[64,128]{1,0:T(8,128)S(1)}, u32[]{:S(2)}) copy-start(f32[64,128]{1,0:T(8,128)S(1)} %get-tuple-element.559) | copy-start | bytes 98308
  107.7 299.1 %all-gather.16.cloned.1.call-start = ((), (), s32[]{:S(2)}) async-start(), calls=%async_computation.12 | async-start | bytes 1179648 | tf_op jit(solution)/shard_map/all_gather | solution.py:184
  178.0 270.4 %all-gather.34.cloned.1.call-start = ((), (), s32[]{:S(2)}) async-start(), calls=%async_computation.21 | async-start | bytes 1179648 | tf_op jit(solution)/shard_map/all_gather | solution.py:183
  178.6 311.6 %all-gather.32.cloned.1.call-start = ((), (), s32[]{:S(2)}) async-start(), calls=%async_computation.20 | async-start | bytes 1179648 | tf_op jit(solution)/shard_map/all_gather | solution.py:184
  182.4 457.7 %all-gather.24.cloned.1.call-start = ((), (), s32[]{:S(2)}) async-start(), calls=%async_computation.16 | async-start | bytes 10485760 | tf_op jit(solution)/shard_map/all_gather | solution.py:59
  183.2 882.0 %all-gather.26.cloned.1.call-start = ((), (), s32[]{:S(2)}) async-start(), calls=%async_computation.17 | async-start | bytes 31457280 | tf_op jit(solution)/shard_map/all_gather | solution.py:68
  183.9 1306.1 %all-gather.28.cloned.1.call-start = ((), (), s32[]{:S(2)}) async-start(), calls=%async_computation.18 | async-start | bytes 31457280 | tf_op jit(solution)/shard_map/all_gather | solution.py:69
  184.5 1730.5 %all-gather.30.cloned.1.call-start = ((), (), s32[]{:S(2)}) async-start(), calls=%async_computation.19 | async-start | bytes 31457280 | tf_op jit(solution)/shard_map/all_gather | solution.py:70
  185.3 1978.6 %reduce-scatter.18.cloned.1.call-start = ((), (), s32[]{:S(2)}) async-start(), calls=%async_computation.25 | async-start | bytes 1179648 | tf_op jit(solution)/shard_map/reduce_scatter | solution.py:235
  2099.2 129.5 %reduce-scatter.14.cloned.1.call-start = ((), (), s32[]{:S(2)}) async-start(), calls=%async_computation.23 | async-start | bytes 1179648 | tf_op jit(solution)/shard_map/reduce_scatter | solution.py:235
  2162.6 132.7 %reduce-scatter.16.cloned.1.call-start = ((), (), s32[]{:S(2)}) async-start(), calls=%async_computation.24 | async-start | bytes 1179648 | tf_op jit(solution)/shard_map/reduce_scatter | solution.py:232
  2163.2 199.2 %reduce-scatter.12.cloned.1.call-start = ((), (), s32[]{:S(2)}) async-start(), calls=%async_computation.22 | async-start | bytes 1179648 | tf_op jit(solution)/shard_map/reduce_scatter | solution.py:232
  2163.8 277.1 %reduce-scatter.24.cloned.1.call-start = ((), (), s32[]{:S(2)}) async-start(), calls=%async_computation.28 | async-start | bytes 5242880 | tf_op jit(solution)/shard_map/reduce_scatter | solution.py:310
  2233.9 287.1 %reduce-scatter.22.cloned.1.call-start = ((), (), s32[]{:S(2)}) async-start(), calls=%async_computation.27 | async-start | bytes 5242880 | tf_op jit(solution)/shard_map/reduce_scatter | solution.py:304
  2371.2 297.6 %reduce-scatter.26.cloned.1.call-start = ((), (), s32[]{:S(2)}) async-start(), calls=%async_computation.29 | async-start | bytes 10485760 | tf_op jit(solution)/shard_map/reduce_scatter | solution.py:316
  2379.0 437.9 %reduce-scatter.20.cloned.1.call-start = ((), (), s32[]{:S(2)}) async-start(), calls=%async_computation.26 | async-start | bytes 10485760 | tf_op jit(solution)/shard_map/reduce_scatter | solution.py:298
  2390.6 843.8 %reduce-scatter.30.cloned.1.call-start = ((), (), s32[]{:S(2)}) async-start(), calls=%async_computation.31 | async-start | bytes 31457280 | tf_op jit(solution)/shard_map/reduce_scatter | solution.py:337
  2404.0 1249.0 %reduce-scatter.28.cloned.1.call-start = ((), (), s32[]{:S(2)}) async-start(), calls=%async_computation.30 | async-start | bytes 31457280 | tf_op jit(solution)/shard_map/reduce_scatter | solution.py:331
  2418.1 1653.6 %reduce-scatter.32.cloned.1.call-start = ((), (), s32[]{:S(2)}) async-start(), calls=%async_computation.32 | async-start | bytes 31457280 | tf_op jit(solution)/shard_map/reduce_scatter | solution.py:343
  2432.3 1958.9 %all-reduce.12.cloned.1.call-start = ((), (), s32[]{:S(2)}) async-start(), calls=%async_computation.33 | async-start | bytes 50331648 | tf_op jit(solution)/shard_map/psum | solution.py:354
  (107 other events, 9973.1 us)
Sparse Core Ops, SparseCore 0:
  9.6 83.6 all-gather.17
  94.9 79.2 all-gather.13
  175.8 148.2 all-gather.21
  326.8 38.4 all-gather.19
  367.8 38.9 all-gather.15
  409.4 38.9 all-gather.33
  451.2 38.9 all-gather.31
  491.7 148.4 all-gather.23
  641.8 423.3 all-gather.25
  1066.6 423.3 all-gather.27
  1491.6 423.3 all-gather.29
  2099.3 62.1 reduce-scatter.17
  2165.9 62.7 reduce-scatter.13
  2232.5 62.7 reduce-scatter.15
  2299.5 62.8 reduce-scatter.11
  2365.1 75.7 reduce-scatter.23
  2443.7 77.2 reduce-scatter.21
  2523.8 144.9 reduce-scatter.25
  2671.7 145.1 reduce-scatter.19
  2819.2 415.1 reduce-scatter.29
  3236.8 416.1 reduce-scatter.27
  3655.4 416.1 reduce-scatter.31
  4077.4 313.7 all-reduce.11
where the time goes:
time: 4440 us; the launch traced here: 4430 us
  waiting for transfers between devices  3820 us (86%)
  matrix products  416 us (9%)
  blocking collectives  66 us (1%)
  other arithmetic  63.2 us (1%)
    reduce_scatter x1, waiting for transfers between devices, shards(): lax.psum_scatter(over_rows(ffn_all, gate_all).astype(jnp.bfloat16), 'shar...  419 us
    reduce_scatter x1, waiting for transfers between devices, shards(): lax.psum_scatter(over_rows(inner_all, cot_all).astype(jnp.bfloat16), 'sha...  419 us
    all_gather x1, waiting for transfers between devices, feedforward_set(): lax.all_gather(w_gate, 'shard', axis=0, tiled=True)  417 us
    reduce_scatter x1, waiting for transfers between devices, shards(): lax.psum_scatter(over_rows(ffn_all, up_all).astype(jnp.bfloat16), 'shard'...  417 us
    all_gather x1, waiting for transfers between devices, feedforward_set(): lax.all_gather(w_up, 'shard', axis=0, tiled=True)  412 us
    all_gather x1, waiting for transfers between devices, feedforward_set(): lax.all_gather(w_down, 'shard', axis=0, tiled=True)  412 us
    psum x1, waiting for transfers between devices, shards(): lax.psum(totals[0].astype(jnp.bfloat16), ('rep', 'ctx')).astype(jnp.float32)  248 us
    reduce_scatter x1, waiting for transfers between devices, shards(): lax.psum_scatter(over_rows(normed_all, dq_all).astype(jnp.bfloat16), 'sha...  148 us
  transfers between devices with their start and end apart: 23, of which 22 were waited for; matrix products, arithmetic and copies ran while one was open for 7% of the time, Pallas kernels for 0%

commit v1 on v0

--- a/solution.py
+++ b/solution.py
@@ -351,7 +351,7 @@
         ).astype(jnp.float32),
     )
     summed = (
-        lax.psum(totals[0].astype(jnp.bfloat16), ("rep", "ctx")).astype(jnp.float32),
+        lax.psum(lax.psum(totals[0].astype(jnp.bfloat16), "ctx"), "rep").astype(jnp.float32),
         lax.psum(totals[1].astype(jnp.bfloat16), ("rep", "ctx")).astype(jnp.float32),
         lax.psum(totals[2].astype(jnp.bfloat16), ("rep", "ctx")).astype(jnp.float32),
         lax.psum(totals[3].astype(jnp.bfloat16), ("rep", "ctx")).astype(jnp.float32),

time: 4440 us -> 4600 us (1.036)
  waiting for transfers between devices: 3820 us -> 3980 us
    reduce_scatter x1, waiting for transfers between devices: 8.33 us -> 80.2 us  [shards(): lax.psum_scatter(over_rows(normed_all, dv_all).astype(jnp.bfloat16), 'sha...]
    reduce_scatter x2, waiting for transfers between devices: 63.3 us -> 123 us  [shards(): lax.psum_scatter(d_values.astype(jnp.bfloat16), ('shard', 'ctx'), scatter...]
    all_gather x2, waiting for transfers between devices: 37 us -> 83.3 us  [shards(): lax.all_gather(key_local, ('shard', 'ctx'), axis=1, tiled=True)]
    psum x1 -> x3, waiting for transfers between devices: 248 us -> 280 us  [the longest x1 270 us: shards(): lax.psum(totals[1].astype(jnp.bfloat16), ('rep', 'ctx')).astype(jnp.float32)]
  transfers between devices with their start and end apart: 23 -> 25, of which waited for: 22 -> 24; matrix products, arithmetic and copies ran while one was open for 7% -> 5% of each run, Pallas kernels for 0% -> 0%
where the time goes in v1:
time: 4600 us; the launch traced here: 4590 us
  waiting for transfers between devices  3980 us (87%)
  matrix products  415 us (9%)
  other arithmetic  68 us (1%)
  blocking collectives  63.1 us (1%)
    reduce_scatter x1, waiting for transfers between devices, shards(): lax.psum_scatter(over_rows(inner_all, cot_all).astype(jnp.bfloat16), 'sha...  419 us
    reduce_scatter x1, waiting for transfers between devices, shards(): lax.psum_scatter(over_rows(ffn_all, up_all).astype(jnp.bfloat16), 'shard'...  419 us
    reduce_scatter x1, waiting for transfers between devices, shards(): lax.psum_scatter(over_rows(ffn_all, gate_all).astype(jnp.bfloat16), 'shar...  418 us
    all_gather x1, waiting for transfers between devices, feedforward_set(): lax.all_gather(w_gate, 'shard', axis=0, tiled=True)  417 us
    all_gather x1, waiting for transfers between devices, feedforward_set(): lax.all_gather(w_up, 'shard', axis=0, tiled=True)  412 us
    all_gather x1, waiting for transfers between devices, feedforward_set(): lax.all_gather(w_down, 'shard', axis=0, tiled=True)  412 us
    psum x1, waiting for transfers between devices, shards(): lax.psum(totals[1].astype(jnp.bfloat16), ('rep', 'ctx')).astype(jnp.float32)  270 us
    reduce_scatter x1, waiting for transfers between devices, shards(): lax.psum_scatter(over_rows(mixed_all, branch_all).astype(jnp.bfloat16), '...  148 us
  transfers between devices with their start and end apart: 25, of which 24 were waited for; matrix products, arithmetic and copies ran while one was open for 5% of the time, Pallas kernels for 0%

profile of v1, /device:TPU:0, one launch (start us, length us, event | category | flops | bytes accessed | tf_op | source)
XLA Modules:
  0.0 4592.7 jit_solution(13012239012973805099)
XLA Ops:
  36.5 56.9 %all-gather.14.cloned.1.call-done = bf16[2048,1024]{1,0:T(8,128)(2,1)} async-done(((bf16[512,1024]{1,0:T(8,128)(2,1)}), bf16[2048,1024]{1,0:T(8,128)(2,1)}) %all-gather.14.cloned.1.call-update) | async-done | bytes 4194320 | tf_op jit(solution)/shard_map/all_gather | solution.py:58
  97.1 77.2 %all-gather.18.cloned.1.call-done = bf16[2048,1024]{1,0:T(8,128)(2,1)} async-done(((bf16[512,1024]{1,0:T(8,128)(2,1)}), bf16[2048,1024]{1,0:T(8,128)(2,1)}) %all-gather.18.cloned.1.call-update) | async-done | bytes 4194320 | tf_op jit(solution)/shard_map/all_gather | solution.py:57
  213.3 110.8 %all-gather.22.cloned.1.call-done = bf16[2048,2048]{1,0:T(8,128)(2,1)} async-done(((bf16[512,2048]{1,0:T(8,128)(2,1)}), bf16[2048,2048]{1,0:T(8,128)(2,1)}) %all-gather.22.cloned.1.call-update) | async-done | bytes 8388624 | tf_op jit(solution)/shard_map/all_gather | solution.py:56
  365.2 41.6 all-gather.34.cloned.1.call-done
  448.4 41.7 all-gather.20.cloned.1.call-done
  490.1 21.6 while.56
  512.2 127.9 %all-gather.24.cloned.1.call-done = bf16[2048,2048]{1,0:T(8,128)(2,1)} async-done(((bf16[512,2048]{1,0:T(8,128)(2,1)}), bf16[2048,2048]{1,0:T(8,128)(2,1)}) %all-gather.24.cloned.1.call-update) | async-done | bytes 8388624 | tf_op jit(solution)/shard_map/all_gather | solution.py:59
  647.8 417.4 %all-gather.26.cloned.1.call-done = bf16[2048,6144]{1,0:T(8,128)(2,1)} async-done(((bf16[512,6144]{1,0:T(8,128)(2,1)}), bf16[2048,6144]{1,0:T(8,128)(2,1)}) %all-gather.26.cloned.1.call-update) | async-done | bytes 25165840 | tf_op jit(solution)/shard_map/all_gather | solution.py:68
  1078.3 411.7 %all-gather.28.cloned.1.call-done = bf16[2048,6144]{1,0:T(8,128)(2,1)} async-done(((bf16[512,6144]{1,0:T(8,128)(2,1)}), bf16[2048,6144]{1,0:T(8,128)(2,1)}) %all-gather.28.cloned.1.call-update) | async-done | bytes 25165840 | tf_op jit(solution)/shard_map/all_gather | solution.py:69
  1503.4 411.6 %all-gather.30.cloned.1.call-done = bf16[6144,2048]{1,0:T(8,128)(2,1)} async-done(((bf16[1536,2048]{1,0:T(8,128)(2,1)}), bf16[6144,2048]{1,0:T(8,128)(2,1)}) %all-gather.30.cloned.1.call-update) | async-done | bytes 25165840 | tf_op jit(solution)/shard_map/all_gather | solution.py:70
  2034.3 55.2 %while.58 = (s32[]{:T(128)}, f32[8,64,2,128]{3,1,2,0:T(8,128)S(1)}, bf16[8,512,128]{2,1,0:T(8,128)(2,1)}, bf16[8,512,128]{2,1,0:T(8,128)(2,1)}, bf16[8,512,128]{...) while((s32[]{:T(128)}, f32[8,64,2,128]{3,1,2,0:T(8,128)S(1)}, ...), condition=%wide.region_19.20_spmd.clone, body=%wide.region_17.19_spmd.clone.sunk | while | flops 84656000 | bytes 3154377 | solution.py:224
  2102.3 55.4 %while.59 = (s32[]{:T(128)}, f32[8,64,2,128]{3,1,2,0:T(8,128)S(1)}, bf16[8,512,128]{2,1,0:T(8,128)(2,1)}, bf16[8,512,128]{2,1,0:T(8,128)(2,1)}, bf16[8,512,128]{...) while((s32[]{:T(128)}, f32[8,64,2,128]{3,1,2,0:T(8,128)S(1)}, ...), condition=%wide.region_28.29_spmd.clone, body=%wide.region_26.28_spmd.clone.sunk | while | flops 84656000 | bytes 3154377 | solution.py:224
  2171.9 140.2 %reduce-scatter.20.cloned.1.call-done = bf16[512,2048]{1,0:T(8,128)(2,1)} async-done(((bf16[2048,2048]{1,0:T(8,128)(2,1)}), bf16[512,2048]{1,0:T(8,128)(2,1)}) %reduce-scatter.20.cloned.1.call-update) | async-done | bytes 2097168 | tf_op jit(solution)/shard_map/reduce_scatter | solution.py:298
  2312.2 68.6 %reduce-scatter.12.cloned.1.call-done = bf16[8,64,128]{2,1,0:T(8,128)(2,1)} async-done(((bf16[8,512,128]{2,1,0:T(8,128)(2,1)}), bf16[8,64,128]{2,1,0:T(8,128)(2,1)}) %reduce-scatter.12.cloned.1.call-update) | async-done | bytes 131088 | tf_op jit(solution)/shard_map/reduce_scatter | solution.py:232
  2380.8 67.2 %reduce-scatter.16.cloned.1.call-done = bf16[8,64,128]{2,1,0:T(8,128)(2,1)} async-done(((bf16[8,512,128]{2,1,0:T(8,128)(2,1)}), bf16[8,64,128]{2,1,0:T(8,128)(2,1)}) %reduce-scatter.16.cloned.1.call-update) | async-done | bytes 131088 | tf_op jit(solution)/shard_map/reduce_scatter | solution.py:232
  2456.7 57.9 %reduce-scatter.18.cloned.1.call-done = bf16[8,64,128]{2,1,0:T(8,128)(2,1)} async-done(((bf16[8,512,128]{2,1,0:T(8,128)(2,1)}), bf16[8,64,128]{2,1,0:T(8,128)(2,1)}) %reduce-scatter.18.cloned.1.call-update) | async-done | bytes 131088 | tf_op jit(solution)/shard_map/reduce_scatter | solution.py:235
  2516.2 65.5 %reduce-scatter.14.cloned.1.call-done = bf16[8,64,128]{2,1,0:T(8,128)(2,1)} async-done(((bf16[8,512,128]{2,1,0:T(8,128)(2,1)}), bf16[8,64,128]{2,1,0:T(8,128)(2,1)}) %reduce-scatter.14.cloned.1.call-update) | async-done | bytes 131088 | tf_op jit(solution)/shard_map/reduce_scatter | solution.py:235
  2645.8 79.5 %reduce-scatter.22.cloned.1.call-done = bf16[512,1024]{1,0:T(8,128)(2,1)} async-done(((bf16[2048,1024]{1,0:T(8,128)(2,1)}), bf16[512,1024]{1,0:T(8,128)(2,1)}) %reduce-scatter.22.cloned.1.call-update) | async-done | bytes 1048592 | tf_op jit(solution)/shard_map/reduce_scatter | solution.py:304
  2725.4 80.2 %reduce-scatter.24.cloned.1.call-done = bf16[512,1024]{1,0:T(8,128)(2,1)} async-done(((bf16[2048,1024]{1,0:T(8,128)(2,1)}), bf16[512,1024]{1,0:T(8,128)(2,1)}) %reduce-scatter.24.cloned.1.call-update) | async-done | bytes 1048592 | tf_op jit(solution)/shard_map/reduce_scatter | solution.py:310
  2805.5 147.9 %reduce-scatter.26.cloned.1.call-done = bf16[512,2048]{1,0:T(8,128)(2,1)} async-done(((bf16[2048,2048]{1,0:T(8,128)(2,1)}), bf16[512,2048]{1,0:T(8,128)(2,1)}) %reduce-scatter.26.cloned.1.call-update) | async-done | bytes 2097168 | tf_op jit(solution)/shard_map/reduce_scatter | solution.py:316
  2953.4 417.6 %reduce-scatter.28.cloned.1.call-done = bf16[512,6144]{1,0:T(8,128)(2,1)} async-done(((bf16[2048,6144]{1,0:T(8,128)(2,1)}), bf16[512,6144]{1,0:T(8,128)(2,1)}) %reduce-scatter.28.cloned.1.call-update) | async-done | bytes 6291472 | tf_op jit(solution)/shard_map/reduce_scatter | solution.py:331
  3371.1 418.6 %reduce-scatter.30.cloned.1.call-done = bf16[512,6144]{1,0:T(8,128)(2,1)} async-done(((bf16[2048,6144]{1,0:T(8,128)(2,1)}), bf16[512,6144]{1,0:T(8,128)(2,1)}) %reduce-scatter.30.cloned.1.call-update) | async-done | bytes 6291472 | tf_op jit(solution)/shard_map/reduce_scatter | solution.py:337
  3789.7 418.7 %reduce-scatter.32.cloned.1.call-done = bf16[1536,2048]{1,0:T(8,128)(2,1)} async-done(((bf16[6144,2048]{1,0:T(8,128)(2,1)}), bf16[1536,2048]{1,0:T(8,128)(2,1)}) %reduce-scatter.32.cloned.1.call-update) | async-done | bytes 6291472 | tf_op jit(solution)/shard_map/reduce_scatter | solution.py:343
  4288.1 270.2 %all-reduce.18.cloned.1.call-done = (bf16[512,1024]{1,0:T(8,128)(2,1)}, bf16[512,1024]{1,0:T(8,128)(2,1)}, bf16[512,2048]{1,0:T(8,128)(2,1)}, bf16[512,6144]{1,0...) async-done(((bf16[512,1024]{1,0:T(8,128)(2,1)}, bf16[512,1024]{1,0:T(8,128)(2,1)}, bf16[512,2048]{1,0:T(8,128)(2,1)}, bf16[512,6144]{1,0:T(8,128)(2,1)}, ...) | async-done | bytes 23068688 | tf_op jit(solution)/shard_map/psum | solution.py:355
  (585 shorter events, 664.9 us)
Async XLA Ops:
  8.0 166.3 %all-gather.18.cloned.1.call-start = ((), (), s32[]{:S(2)}) async-start(), calls=%async_computation.13 | async-start | bytes 5242880 | tf_op jit(solution)/shard_map/all_gather | solution.py:57
  8.7 315.4 %all-gather.22.cloned.1.call-start = ((), (), s32[]{:S(2)}) async-start(), calls=%async_computation.15 | async-start | bytes 10485760 | tf_op jit(solution)/shard_map/all_gather | solution.py:56
  9.5 355.8 %all-gather.32.cloned.1.call-start = ((), (), s32[]{:S(2)}) async-start(), calls=%async_computation.20 | async-start | bytes 1179648 | tf_op jit(solution)/shard_map/all_gather | solution.py:184
  180.7 226.1 %all-gather.34.cloned.1.call-start = ((), (), s32[]{:S(2)}) async-start(), calls=%async_computation.21 | async-start | bytes 1179648 | tf_op jit(solution)/shard_map/all_gather | solution.py:183
  189.0 259.4 %all-gather.16.cloned.1.call-start = ((), (), s32[]{:S(2)}) async-start(), calls=%async_computation.12 | async-start | bytes 1179648 | tf_op jit(solution)/shard_map/all_gather | solution.py:184
  192.8 297.4 %all-gather.20.cloned.1.call-start = ((), (), s32[]{:S(2)}) async-start(), calls=%async_computation.14 | async-start | bytes 1179648 | tf_op jit(solution)/shard_map/all_gather | solution.py:183
  193.5 446.6 %all-gather.24.cloned.1.call-start = ((), (), s32[]{:S(2)}) async-start(), calls=%async_computation.16 | async-start | bytes 10485760 | tf_op jit(solution)/shard_map/all_gather | solution.py:59
  194.3 870.9 %all-gather.26.cloned.1.call-start = ((), (), s32[]{:S(2)}) async-start(), calls=%async_computation.17 | async-start | bytes 31457280 | tf_op jit(solution)/shard_map/all_gather | solution.py:68
  195.0 1295.0 %all-gather.28.cloned.1.call-start = ((), (), s32[]{:S(2)}) async-start(), calls=%async_computation.18 | async-start | bytes 31457280 | tf_op jit(solution)/shard_map/all_gather | solution.py:69
  195.6 1719.3 %all-gather.30.cloned.1.call-start = ((), (), s32[]{:S(2)}) async-start(), calls=%async_computation.19 | async-start | bytes 31457280 | tf_op jit(solution)/shard_map/all_gather | solution.py:70
  196.4 2115.7 %reduce-scatter.20.cloned.1.call-start = ((), (), s32[]{:S(2)}) async-start(), calls=%async_computation.26 | async-start | bytes 10485760 | tf_op jit(solution)/shard_map/reduce_scatter | solution.py:298
  2169.3 211.4 %reduce-scatter.12.cloned.1.call-start = ((), (), s32[]{:S(2)}) async-start(), calls=%async_computation.22 | async-start | bytes 1179648 | tf_op jit(solution)/shard_map/reduce_scatter | solution.py:232
  2170.1 277.8 %reduce-scatter.16.cloned.1.call-start = ((), (), s32[]{:S(2)}) async-start(), calls=%async_computation.24 | async-start | bytes 1179648 | tf_op jit(solution)/shard_map/reduce_scatter | solution.py:232
  2170.7 343.9 %reduce-scatter.18.cloned.1.call-start = ((), (), s32[]{:S(2)}) async-start(), calls=%async_computation.25 | async-start | bytes 1179648 | tf_op jit(solution)/shard_map/reduce_scatter | solution.py:235
  2171.3 410.4 %reduce-scatter.14.cloned.1.call-start = ((), (), s32[]{:S(2)}) async-start(), calls=%async_computation.23 | async-start | bytes 1179648 | tf_op jit(solution)/shard_map/reduce_scatter | solution.py:235
  2171.8 473.9 %all-reduce.14.cloned.1.call-start = ((), (), s32[]{:S(2)}) async-start(), calls=%async_computation.27 | async-start | bytes 4194304 | tf_op jit(solution)/shard_map/psum | solution.py:354
  2312.1 413.2 %reduce-scatter.22.cloned.1.call-start = ((), (), s32[]{:S(2)}) async-start(), calls=%async_computation.29 | async-start | bytes 5242880 | tf_op jit(solution)/shard_map/reduce_scatter | solution.py:304
  2456.7 348.9 %reduce-scatter.24.cloned.1.call-start = ((), (), s32[]{:S(2)}) async-start(), calls=%async_computation.30 | async-start | bytes 5242880 | tf_op jit(solution)/shard_map/reduce_scatter | solution.py:310
  2587.0 366.4 %reduce-scatter.26.cloned.1.call-start = ((), (), s32[]{:S(2)}) async-start(), calls=%async_computation.31 | async-start | bytes 10485760 | tf_op jit(solution)/shard_map/reduce_scatter | solution.py:316
  2594.2 776.9 %reduce-scatter.28.cloned.1.call-start = ((), (), s32[]{:S(2)}) async-start(), calls=%async_computation.32 | async-start | bytes 31457280 | tf_op jit(solution)/shard_map/reduce_scatter | solution.py:331
  2608.0 1181.7 %reduce-scatter.30.cloned.1.call-start = ((), (), s32[]{:S(2)}) async-start(), calls=%async_computation.33 | async-start | bytes 31457280 | tf_op jit(solution)/shard_map/reduce_scatter | solution.py:337
  2621.6 1586.8 %reduce-scatter.32.cloned.1.call-start = ((), (), s32[]{:S(2)}) async-start(), calls=%async_computation.34 | async-start | bytes 31457280 | tf_op jit(solution)/shard_map/reduce_scatter | solution.py:343
  2636.0 1647.8 %all-reduce.16.cloned.1.call-start = ((), (), s32[]{:S(2)}) async-start(), calls=%async_computation.28 | async-start | bytes 4194304 | tf_op jit(solution)/shard_map/psum | solution.py:354
  2645.8 1912.5 %all-reduce.18.cloned.1.call-start = ((), (), s32[]{:S(2)}) async-start(), calls=%async_computation.35 | async-start | bytes 46137344 | tf_op jit(solution)/shard_map/psum | solution.py:355
  (85 other events, 9873.9 us)
Sparse Core Ops, SparseCore 0:
  9.6 83.6 all-gather.13
  94.9 79.2 all-gather.17
  175.8 148.2 all-gather.21
  367.8 38.9 all-gather.33
  409.4 38.9 all-gather.15
  451.2 38.9 all-gather.19
  491.7 148.3 all-gather.23
  641.7 423.3 all-gather.25
  1066.6 423.3 all-gather.27
  1491.6 423.3 all-gather.29
  2169.4 142.6 reduce-scatter.19
  2316.1 64.6 reduce-scatter.11
  2385.0 62.8 reduce-scatter.15
  2451.7 62.8 reduce-scatter.17
  2518.8 62.8 reduce-scatter.13
  2583.8 61.8 all-reduce.13
  2648.6 76.7 reduce-scatter.21
  2728.2 77.2 reduce-scatter.23
  2808.4 144.9 reduce-scatter.25
  2955.9 415.0 reduce-scatter.27
  3373.4 416.1 reduce-scatter.29
  3792.2 416.1 reduce-scatter.31
  4210.6 53.2 all-reduce.15
  4269.5 288.6 all-reduce.17
  (1 shorter events, 38.4 us)
